TPU v7x, 256 devices: a whole 4x4x8 slice. The times are simulated.
256 devices in a mesh: chan: 64 (over x, y_hi, z), band: 4 (over y_lo, core).
Axes of the slice: x: 4, y: 4 (y_hi: 2, y_lo: 2; y = y_hi * 2 + y_lo), z: 8, core: 2. Of those that a mesh axis runs over, the one named last changes fastest.
Arguments:
- spectra: float32 [2, 32, 96, 8192], P(None, None, 'band', 'chan'), may hold values from -6 to 6
- taps: float32 [96, 16], replicated, may hold values from -2.5 to 2.5
Outputs:
- stacked: bfloat16 [8, 2, 8192, 8192], P('band', None, 'chan')
All inputs are finite; a program needn't handle non-finite values.
Results may differ from a plain program's by a relative error of at most 0.0057.
Values may be sent and summed in bfloat16 or wider, within the bound.
No kernel may reach another device: no remote copies, remote signals or barrier semaphores. Data moves between devices by JAX's collectives and lax.ppermute only.
A program may use at most 192 MiB of HBM per device.

v0:
```python
import jax
import jax.numpy as jnp
from jax import lax
from jax.sharding import PartitionSpec as P

TAPS = 16
SMOOTH = 5
BAND_BINS = 12
water_level = 0.1


def padded(shard, sides, width, wrap):
    for axis, dim in sides:
        devices, length = (lax.axis_size(axis), shard.shape[dim])
        up = [(i, (i + 1) % devices) for i in range(devices if wrap else devices - 1)]
        down = [(j, i) for i, j in up]
        last = lax.slice_in_dim(shard, length - width, length, axis=dim)
        first = lax.slice_in_dim(shard, 0, width, axis=dim)
        before = lax.ppermute(last, axis, up)
        after = lax.ppermute(first, axis, down)
        shard = jnp.concatenate([before, shard, after], axis=dim)
    return shard


def fan_filter(extended, coeffs, width):
    result = jnp.zeros(extended.shape[:-1] + (width,), jnp.float32)
    for tap_index in range(coeffs.shape[1]):
        result = (
            result + coeffs[:, tap_index][:, None] * extended[..., tap_index : tap_index + width]
        )
    return result


def whiten(filtered, amp_ext, local_bins):
    smoothed = jnp.zeros(filtered.shape[1:], jnp.float32)
    for offset in range(SMOOTH):
        smoothed = smoothed + amp_ext[:, offset : offset + local_bins, :]
    smoothed = smoothed / SMOOTH
    return (filtered / (smoothed + water_level)[None]).astype(jnp.bfloat16)


def arrange(whitened, band_count):
    shaped = whitened.reshape(2, whitened.shape[1], band_count, BAND_BINS, whitened.shape[3])
    shaped = shaped.transpose(2, 0, 1, 3, 4)
    return shaped.reshape(band_count, 2 * whitened.shape[1] * BAND_BINS, whitened.shape[3])


def partner(whitened):
    return jnp.concatenate([-whitened[1:2], whitened[0:1]], axis=0)


def body(spectra, taps):
    half_taps = TAPS // 2
    reach = SMOOTH // 2
    local_bins = spectra.shape[2]
    local_chan = spectra.shape[3]
    anchor = lax.axis_index("band") * local_bins
    padded_taps = jnp.pad(taps, ((reach, reach), (0, 0)))
    coeffs = lax.dynamic_slice_in_dim(padded_taps, anchor + reach, local_bins, 0)
    extended = padded(spectra, (("chan", 3),), half_taps, True)
    filtered = fan_filter(extended, coeffs, local_chan)
    amplitude = jnp.sqrt(filtered[0] * filtered[0] + filtered[1] * filtered[1])
    amp_ext = padded(amplitude, (("band", 1),), reach, False)
    whitened = whiten(filtered, amp_ext, local_bins)
    band_count = local_bins // BAND_BINS
    features = arrange(whitened, band_count)
    scale_factor = 1.0 / (whitened.shape[1] * BAND_BINS)
    remote = lax.all_gather(whitened, "chan", axis=3, tiled=True)
    right = arrange(remote, band_count)
    turned = arrange(partner(remote), band_count)
    real_part = jnp.einsum("bki,bkj->bij", features, right, preferred_element_type=jnp.float32)
    imag_part = jnp.einsum("bki,bkj->bij", features, turned, preferred_element_type=jnp.float32)
    return (jnp.stack([real_part, imag_part], axis=1) * scale_factor).astype(jnp.bfloat16)


def solution(mesh):
    placed = (P(None, None, "band", "chan"), P())
    return jax.shard_map(
        body, mesh=mesh, in_specs=placed, out_specs=P("band", None, "chan", None), check_vma=False
    )
```

profile of v0, /device:TPU:8, one launch (start us, length us, event | category | flops | bytes accessed | tf_op | source)
XLA Modules:
  0.0 518.0 jit_solution(13013517061511016048)
XLA Ops:
  6.5 1.6 fusion.81
  8.2 0.3 copy.36
  8.4 9.8 %collective-permute-start.1 = (f32[2,32,24,8]{1,3,2,0:T(8,128)S(1)}, f32[2,32,24,8]{1,3,2,0:T(8,128)S(1)}, u32[]{:S(2)}, u32[]{:S(2)}) collective-permute-start(f32[2,32,24,8]{1,3,2,0:T(8,128)S(1)} %copy.36), channel_id=1, source_target_pairs={{4,0},{8,4},{12,8},{16,12},{20,16},{24,20},{28,24},{32,28},{36,32}... | collective-permute-start | bytes 147464 | tf_op jit(solution)/shard_map/ppermute | solution.py:20
  18.3 0.3 copy.35
  18.5 0.1 collective-permute-start
  18.6 1.1 fusion.66
  19.6 1.0 fusion.67
  20.7 1.3 copy.22
  21.9 8.7 %collective-permute-done = f32[2,32,24,8]{1,3,2,0:T(8,128)S(1)} collective-permute-done((f32[2,32,24,8]{1,3,2,0:T(8,128)S(1)}, f32[2,32,24,8]{1,3,2,0:T(8,128)S(1)}, u32[]{:S(2)}, u32[]{:S(2)}) %collective-permute-start) | collective-permute-done | bytes 49184 | tf_op jit(solution)/shard_map/ppermute | solution.py:19
  30.6 0.3 copy.21
  30.9 0.0 collective-permute-done.1
  31.0 0.3 copy.26
  31.2 6.6 %fusion.14 = f32[2,32,24,128]{3,1,2,0:T(8,128)S(1)} fusion(f32[2,32,24,128]{3,1,2,0:T(8,128)S(1)} %copy.22, f32[2,32,24,8]{3,1,2,0:T(8,128)S(1)} %copy.26, f32[2,32,24,8]{3,1,2,0:T(8,128)S(1)} %copy.21, f32[24]{0:T(128)S(1)} %get-tuple-element.26, f32[24]{0:T(128)S(1)} %get-tuple-element.12, f32[24]{0:T(128)S(1)} %get-tuple-element.13, ...), kind=kLoop, calls=%fused_computation.39 | loop fusion | flops 9043968 | bytes 1672704 | tf_op jit(solution)/shard_map/add | solution.py:29
  37.8 0.1 fusion.64
  38.0 1.9 collective-permute-start.2
  39.9 3.6 collective-permute-start.3
  43.6 0.0 collective-permute-done.2
  43.6 1.6 collective-permute-done.3
  45.1 0.1 fusion.58
  45.2 0.9 divide_convert_fusion
  46.1 0.0 all-gather.2.cloned.1.call-update
  46.1 1.4 copy.27
  47.5 0.4 copy.29
  48.0 227.1 %all-gather.2.cloned.1.call-done = bf16[2,32,24,8192]{3,1,2,0:T(8,128)(2,1)} async-done(((bf16[2,32,24,128]{3,1,2,0:T(8,128)(2,1)}), bf16[2,32,24,8192]{3,1,2,0:T(8,128)(2,1)}) %all-gather.2.cloned.1.call-update) | async-done | bytes 25165840 | tf_op jit(solution)/shard_map/all_gather | solution.py:68
  275.1 46.2 %copy.28 = bf16[2,2,32,12,8192]{4,0,3,2,1:T(2,128)(2,1)} copy(bf16[2,2,32,12,8192]{4,2,3,0,1:T(8,128)(2,1)} %bitcast.52) | data formatting | bytes 50331648 | tf_op jit(solution)/shard_map/transpose | solution.py:44
  321.4 8.7 %slice_negate_fusion = (bf16[1,32,24,8192]{3,1,2,0:T(8,128)(2,1)}, bf16[1,32,24,8192]{3,1,2,0:T(8,128)(2,1)}) fusion(bf16[2,32,24,8192]{3,1,2,0:T(8,128)(2,1)S(1)} %bitcast.54), kind=kLoop, calls=%fused_computation.7 | loop fusion | flops 6291456 | bytes 50331648 | tf_op jit(solution)/shard_map/neg | solution.py:49
  330.1 11.8 %pad_maximum_fusion = bf16[2,32,24,8192]{3,1,2,0:T(8,128)(2,1)S(1)} fusion(bf16[1,32,24,8192]{3,1,2,0:T(8,128)(2,1)} %get-tuple-element.6, bf16[1,32,24,8192]{3,1,2,0:T(8,128)(2,1)} %get-tuple-element.5), kind=kLoop, calls=%fused_computation | loop fusion | flops 12582912 | bytes 50331648 | tf_op jit(solution)/shard_map/concatenate | solution.py:49
  341.9 53.3 %copy.31 = bf16[2,2,32,12,8192]{4,0,3,2,1:T(2,128)(2,1)} copy(bf16[2,2,32,12,8192]{4,2,3,0,1:T(8,128)(2,1)S(1)} %bitcast.57) | data formatting | bytes 50331648 | tf_op jit(solution)/shard_map/transpose | solution.py:44
  395.2 56.0 %fusion.5 = f32[2,1,128,8192]{3,2,0,1:T(8,128)S(1)} fusion(bf16[2,768,128]{1,2,0:T(8,128)(2,1)S(1)} %copy.29, bf16[2,768,8192]{2,0,1:T(2,128)(2,1)} %bitcast.55), kind=kOutput, calls=%fused_computation.8 | convolution fusion | flops 3221225472 | bytes 33947648 | tf_op jit(solution)/shard_map/bki,bkj->bij/dot_general | solution.py:71
  451.2 44.2 %fusion.8 = f32[2,1,128,8192]{3,2,0,1:T(8,128)} fusion(bf16[2,768,128]{1,2,0:T(8,128)(2,1)S(1)} %copy.29, bf16[2,768,8192]{2,0,1:T(2,128)(2,1)} %bitcast.56), kind=kOutput, calls=%fused_computation.9 | convolution fusion | flops 3221225472 | bytes 33947648 | tf_op jit(solution)/shard_map/bki,bkj->bij/dot_general | solution.py:72
  495.4 7.8 %fusion.4 = bf16[2,2,128,8192]{3,2,0,1:T(8,128)(2,1)} fusion(f32[2,1,128,8192]{3,2,0,1:T(8,128)} %fusion.8, f32[2,1,128,8192]{3,2,0,1:T(8,128)S(1)} %fusion.5), kind=kLoop, calls=%fused_computation.6 | loop fusion | flops 12582912 | bytes 25165824 | tf_op jit(solution)/shard_map/convert_element_type | solution.py:73
  503.2 7.8 %copy.34 = bf16[2,2,128,8192]{3,2,1,0:T(8,128)(2,1)} copy(bf16[2,2,128,8192]{3,2,0,1:T(8,128)(2,1)} %fusion.4) | data formatting | bytes 16777216 | tf_op jit(solution)/shard_map/convert_element_type | solution.py:73
  (15 shorter events, 0.0 us)
Async XLA Ops:
  6.5 268.6 %all-gather.2.cloned.1.call-start = ((), (), s32[]{:S(2)}) async-start(), calls=%async_computation | async-start | bytes 25559040 | tf_op jit(solution)/shard_map/all_gather | solution.py:68
  8.4 22.5 %collective-permute-start.1 = (f32[2,32,24,8]{1,3,2,0:T(8,128)S(1)}, f32[2,32,24,8]{1,3,2,0:T(8,128)S(1)}, u32[]{:S(2)}, u32[]{:S(2)}) collective-permute-start(f32[2,32,24,8]{1,3,2,0:T(8,128)S(1)} %copy.36), channel_id=1, source_target_pairs={{4,0},{8,4},{12,8},{16,12},{20,16},{24,20},{28,24},{32,28},{36,32}... | collective-permute-start | bytes 147464 | tf_op jit(solution)/shard_map/ppermute | solution.py:20
  18.5 12.1 %collective-permute-start = (f32[2,32,24,8]{1,3,2,0:T(8,128)S(1)}, f32[2,32,24,8]{1,3,2,0:T(8,128)S(1)}, u32[]{:S(2)}, u32[]{:S(2)}) collective-permute-start(f32[2,32,24,8]{1,3,2,0:T(8,128)S(1)} %copy.35), channel_id=1, source_target_pairs={{0,4},{4,8},{8,12},{12,16},{16,20},{20,24},{24,28},{28,32},{32,36}... | collective-permute-start | bytes 147464 | tf_op jit(solution)/shard_map/ppermute | solution.py:19
  38.0 5.6 %collective-permute-start.2 = (f32[32,2,128]{2,0,1:T(8,128)S(1)}, f32[32,2,128]{2,0,1:T(8,128)S(1)}, u32[]{:S(2)}, u32[]{:S(2)}) collective-permute-start(f32[32,2,128]{2,0,1:T(8,128)S(1)} %get-tuple-element.9), channel_id=1, source_target_pairs={{0,1},{1,2},{2,3},{4,5},{5,6},{6,7},{8,9},{9,10},{10,11},{12,13},{... | collective-permute-start | bytes 98312 | tf_op jit(solution)/shard_map/ppermute | solution.py:19
  39.9 5.2 %collective-permute-start.3 = (f32[32,2,128]{2,0,1:T(8,128)S(1)}, f32[32,2,128]{2,0,1:T(8,128)S(1)}, u32[]{:S(2)}, u32[]{:S(2)}) collective-permute-start(f32[32,2,128]{2,0,1:T(8,128)S(1)} %get-tuple-element.10), channel_id=1, source_target_pairs={{1,0},{2,1},{3,2},{5,4},{6,5},{7,6},{9,8},{10,9},{11,10},{13,12},{... | collective-permute-start | bytes 98312 | tf_op jit(solution)/shard_map/ppermute | solution.py:20
  275.1 46.2 %slice-start = ((s8[25165824]{0:T(1024)(128)(4,1)}), s8[4194304]{0:T(1024)(128)(4,1)S(1)}, s32[]{:S(2)}) async-start(s8[25165824]{0:T(1024)(128)(4,1)} %bitcast.53), calls=%async_computation.1 | async-start | bytes 8388608
  275.1 46.2 %slice-start.1 = ((s8[25165824]{0:T(1024)(128)(4,1)}), s8[4194304]{0:T(1024)(128)(4,1)S(1)}, s32[]{:S(2)}) async-start(s8[25165824]{0:T(1024)(128)(4,1)} %bitcast.53), calls=%async_computation.2 | async-start | bytes 8388608
  275.1 46.2 %slice-start.2 = ((s8[25165824]{0:T(1024)(128)(4,1)}), s8[4194304]{0:T(1024)(128)(4,1)S(1)}, s32[]{:S(2)}) async-start(s8[25165824]{0:T(1024)(128)(4,1)} %bitcast.53), calls=%async_computation.3 | async-start | bytes 8388608
  275.1 46.2 %slice-start.3 = ((s8[25165824]{0:T(1024)(128)(4,1)}), s8[4194304]{0:T(1024)(128)(4,1)S(1)}, s32[]{:S(2)}) async-start(s8[25165824]{0:T(1024)(128)(4,1)} %bitcast.53), calls=%async_computation.4 | async-start | bytes 8388608
  275.1 46.3 %slice-start.4 = ((s8[25165824]{0:T(1024)(128)(4,1)}), s8[4194304]{0:T(1024)(128)(4,1)S(1)}, s32[]{:S(2)}) async-start(s8[25165824]{0:T(1024)(128)(4,1)} %bitcast.53), calls=%async_computation.5 | async-start | bytes 8388608
  275.1 46.3 %slice-start.5 = ((s8[25165824]{0:T(1024)(128)(4,1)}), s8[4194304]{0:T(1024)(128)(4,1)S(1)}, s32[]{:S(2)}) async-start(s8[25165824]{0:T(1024)(128)(4,1)} %bitcast.53), calls=%async_computation.6 | async-start | bytes 8388608
Sparse Core Ops, SparseCore 0:
  46.3 228.7 all-gather.1
where the time goes:
time: 525 us; the launch traced here: 518 us
  waiting for transfers between devices  237 us (45%)
  local copies, waits for them, and re-layouts  115 us (22%)
  matrix products  100 us (19%)
  other arithmetic  35.9 us (7%)
  starting transfers between devices  15.4 us (3%)
  between operations  13.8 us (3%)
    all_gather x1, waiting for transfers between devices, body(): remote = lax.all_gather(whitened, 'chan', axis=3, tiled=True)  227 us
    transpose x3, local copies, waits for them, and re-layouts, arrange(): shaped = shaped.transpose(2, 0, 1, 3, 4)  101 us
    dot_general x1, matrix products, body(): jnp.einsum('bki,bkj->bij', features, right, preferred_element_type=jnp.fl...  56 us
    dot_general x1, matrix products, body(): jnp.einsum('bki,bkj->bij', features, turned, preferred_element_type=jnp.f...  44.2 us
    ppermute x2, starting transfers between devices, padded(): after = lax.ppermute(first, axis, down)  13.5 us
    concatenate x1, other arithmetic, partner(): return jnp.concatenate([-whitened[1:2], whitened[0:1]], axis=0)  11.8 us
  transfers between devices with their start and end apart: 5, of which 3 were waited for; matrix products, arithmetic and copies ran while one was open for 1% of the time, Pallas kernels for 0%

commit v1 on v0

--- a/solution.py
+++ b/solution.py
@@ -7,6 +7,19 @@
 SMOOTH = 5
 BAND_BINS = 12
 water_level = 0.1
+
+
+def record_tell(in_array, shard_axis):
+    local_out = jnp.concatenate(
+        lax.all_to_all(
+            jnp.stack(lax.axis_size(shard_axis) * [in_array], axis=0),
+            axis_name=shard_axis,
+            split_axis=0,
+            concat_axis=0,
+        ),
+        3,
+    )
+    return local_out
 
 
 def padded(shard, sides, width, wrap):
@@ -65,7 +78,7 @@
     band_count = local_bins // BAND_BINS
     features = arrange(whitened, band_count)
     scale_factor = 1.0 / (whitened.shape[1] * BAND_BINS)
-    remote = lax.all_gather(whitened, "chan", axis=3, tiled=True)
+    remote = record_tell(whitened, "chan")
     right = arrange(remote, band_count)
     turned = arrange(partner(remote), band_count)
     real_part = jnp.einsum("bki,bkj->bij", features, right, preferred_element_type=jnp.float32)

time: 525 us -> 1030 us (1.96)
  the two profiles are of different devices: /device:TPU:8 before, /device:TPU:101 now
where the time goes in v1:
time: 1030 us; the launch traced here: 1020 us
  waiting for transfers between devices  602 us (58%)
  local copies, waits for them, and re-layouts  250 us (24%)
  matrix products  100 us (10%)
  other arithmetic  43.8 us (4%)
  starting transfers between devices  28.8 us (3%)
    all_to_all x1, waiting for transfers between devices, record_tell(): lax.all_to_all(jnp.stack(lax.axis_size(shard_axis) * [in_array], axis=0),...  598 us
    transpose x3, local copies, waits for them, and re-layouts, arrange(): shaped = shaped.transpose(2, 0, 1, 3, 4)  100 us
    dot_general x1, matrix products, body(): jnp.einsum('bki,bkj->bij', features, right, preferred_element_type=jnp.fl...  56 us
    dot_general x1, matrix products, body(): jnp.einsum('bki,bkj->bij', features, turned, preferred_element_type=jnp.f...  44.2 us
    another operation x1, local copies, waits for them, and re-layouts, arrange(): whitened.reshape(2, whitened.shape[1], band_count, BAND_BINS, whitened.sh...  37.3 us
    neg x2, local copies, waits for them, and re-layouts, partner(): return jnp.concatenate([-whitened[1:2], whitened[0:1]], axis=0)  28.5 us
    reshape x1, local copies, waits for them, and re-layouts, record_tell(): jnp.concatenate(lax.all_to_all(jnp.stack(lax.axis_size(shard_axis) * [in_...  26.8 us
  transfers between devices with their start and end apart: 5, of which 4 were waited for; matrix products, arithmetic and copies ran while one was open for 0% of the time, Pallas kernels for 0%

profile of v1, /device:TPU:101, one launch (start us, length us, event | category | flops | bytes accessed | tf_op | source)
XLA Modules:
  0.0 1024.6 jit_solution(16063989296478815750)
XLA Ops:
  0.0 1.7 fusion.81
  1.7 0.3 copy.37
  2.3 2.9 collective-permute-start
  5.2 1.0 fusion.66
  6.2 1.0 fusion.67
  7.2 1.3 copy.20
  8.7 0.3 copy.19
  8.9 0.4 collective-permute-done.1
  9.4 0.3 copy.24
  9.6 6.6 fusion.14
  16.4 4.4 collective-permute-start.2
  20.8 1.9 collective-permute-start.3
  22.8 3.3 collective-permute-done.3
  26.3 9.0 stack.8
  35.3 19.5 %all-to-all-start = ((bf16[64,2,32,24,128]{4,2,3,1,0:T(8,128)(2,1)}), bf16[64,2,32,24,128]{4,2,3,1,0:T(8,128)(2,1)}, u32[]{:S(2)}, u32[]{:S(2)}) async-start(bf16[64,2,32,24,128]{4,2,3,1,0:T(8,128)(2,1)} %stack.8), calls=%async_computation | async-start | bytes 50331648 | tf_op jit(solution)/shard_map/all_to_all | solution.py:14
  54.8 0.4 copy.25
  55.2 0.4 copy.28
  55.7 598.0 %all-to-all-done = bf16[64,2,32,24,128]{4,2,3,1,0:T(8,128)(2,1)} async-done(((bf16[64,2,32,24,128]{4,2,3,1,0:T(8,128)(2,1)}), bf16[64,2,32,24,128]{4,2,3,1,0:T(8,128)(2,1)}, u32[]{:S(2)}, u32[]{:S(2)}) %all-to-all-start) | async-done | bytes 25165856 | tf_op jit(solution)/shard_map/all_to_all | solution.py:14
  653.7 26.8 %copy.26 = bf16[2,32,24,64,128]{4,3,1,2,0:T(8,128)(2,1)} copy(bf16[2,32,24,64,128]{4,1,2,0,3:T(8,128)(2,1)} %bitcast.20) | data formatting | bytes 50331648 | tf_op jit(solution)/shard_map/reshape | solution.py:13
  680.5 17.4 %slice_negate_fusion = (bf16[1,32,24,64,128]{4,1,2,0,3:T(8,128)(2,1)}, bf16[1,32,24,64,128]{4,1,2,0,3:T(8,128)(2,1)}) fusion(bf16[2,32,24,64,128]{4,1,2,0,3:T(8,128)(2,1)} %bitcast.20), kind=kLoop, calls=%fused_computation.7 | loop fusion | flops 6291456 | bytes 50331648 | tf_op jit(solution)/shard_map/neg | solution.py:62
  697.9 37.3 %reshape_reshape.3 = bf16[2,32,2,12,8192]{4,1,3,2,0:T(8,128)(2,1)} reshape(bf16[2,32,24,64,128]{4,3,1,2,0:T(8,128)(2,1)} %copy.26) | data formatting | bytes 50331648 | tf_op jit(solution)/shard_map/reshape;reshape | solution.py:56
  735.2 46.2 %copy.27 = bf16[2,2,32,12,8192]{4,0,3,2,1:T(2,128)(2,1)} copy(bf16[2,2,32,12,8192]{4,2,3,0,1:T(8,128)(2,1)} %bitcast.64) | data formatting | bytes 50331648 | tf_op jit(solution)/shard_map/transpose | solution.py:57
  781.4 9.2 copy.30
  790.7 19.3 %neg.16 = bf16[1,32,2,12,8192]{4,1,3,2,0:T(8,128)(2,1)} reshape(bf16[1,32,24,64,128]{4,3,1,2,0:T(8,128)(2,1)} %copy.30) | data formatting | bytes 25165824 | tf_op jit(solution)/shard_map/neg | solution.py:62
  809.9 14.4 %copy.31 = bf16[1,32,24,64,128]{4,3,1,2,0:T(8,128)(2,1)} copy(bf16[1,32,24,64,128]{4,1,2,0,3:T(8,128)(2,1)} %get-tuple-element.6) | data formatting | bytes 25165824 | tf_op jit(solution)/shard_map/slice | solution.py:62
  824.4 19.3 %concatenate.39 = bf16[1,32,2,12,8192]{4,1,3,2,0:T(8,128)(2,1)} reshape(bf16[1,32,24,64,128]{4,3,1,2,0:T(8,128)(2,1)} %copy.31) | data formatting | bytes 25165824 | tf_op jit(solution)/shard_map/concatenate | solution.py:62
  843.7 11.8 %maximum_bitcast_fusion = bf16[2,2,32,12,8192]{4,2,3,0,1:T(8,128)(2,1)S(1)} fusion(bf16[1,32,2,12,8192]{4,1,3,2,0:T(8,128)(2,1)} %concatenate.39, bf16[1,32,2,12,8192]{4,1,3,2,0:T(8,128)(2,1)} %neg.16), kind=kLoop, calls=%fused_computation | loop fusion | flops 12582912 | bytes 50331648 | tf_op jit(solution)/shard_map/transpose | solution.py:57
  855.5 53.4 %copy.32 = bf16[2,2,32,12,8192]{4,0,3,2,1:T(2,128)(2,1)} copy(bf16[2,2,32,12,8192]{4,2,3,0,1:T(8,128)(2,1)S(1)} %maximum_bitcast_fusion) | data formatting | bytes 50331648 | tf_op jit(solution)/shard_map/transpose | solution.py:57
  908.8 56.0 %fusion.5 = f32[2,1,128,8192]{3,2,0,1:T(8,128)S(1)} fusion(bf16[2,768,128]{1,2,0:T(8,128)(2,1)S(1)} %copy.28, bf16[2,768,8192]{2,0,1:T(2,128)(2,1)} %bitcast.62), kind=kOutput, calls=%fused_computation.8 | convolution fusion | flops 3221225472 | bytes 33947648 | tf_op jit(solution)/shard_map/bki,bkj->bij/dot_general | solution.py:84
  964.8 44.2 %fusion.8 = f32[2,1,128,8192]{3,2,0,1:T(8,128)} fusion(bf16[2,768,128]{1,2,0:T(8,128)(2,1)S(1)} %copy.28, bf16[2,768,8192]{2,0,1:T(2,128)(2,1)} %bitcast.63), kind=kOutput, calls=%fused_computation.9 | convolution fusion | flops 3221225472 | bytes 33947648 | tf_op jit(solution)/shard_map/bki,bkj->bij/dot_general | solution.py:85
  1009.0 7.7 fusion.4
  1016.6 7.8 copy.35
  (10 shorter events, 0.8 us)
Async XLA Ops:
  2.0 7.4 collective-permute-start.1
  2.3 6.4 collective-permute-start
  16.4 6.4 collective-permute-start.2
  20.8 5.2 collective-permute-start.3
  35.3 618.4 %all-to-all-start = ((bf16[64,2,32,24,128]{4,2,3,1,0:T(8,128)(2,1)}), bf16[64,2,32,24,128]{4,2,3,1,0:T(8,128)(2,1)}, u32[]{:S(2)}, u32[]{:S(2)}) async-start(bf16[64,2,32,24,128]{4,2,3,1,0:T(8,128)(2,1)} %stack.8), calls=%async_computation | async-start | bytes 50331648 | tf_op jit(solution)/shard_map/all_to_all | solution.py:14
  735.2 46.2 %copy-start = (bf16[1,32,24,64,128]{4,1,2,0,3:T(8,128)(2,1)S(1)}, bf16[1,32,24,64,128]{4,1,2,0,3:T(8,128)(2,1)}, u32[]{:S(2)}) copy-start(bf16[1,32,24,64,128]{4,1,2,0,3:T(8,128)(2,1)} %get-tuple-element.5) | copy-start | bytes 37748740
